TPU v7x, 32 devices: a whole 2x2x4 slice. The times are simulated.
32 devices in a mesh: cell: 8 (over y, x, core), chan: 4 (over z).
Axes of the slice: x: 2, y: 2, z: 4, core: 2. Of those that a mesh axis runs over, the one named last changes fastest.
Arguments:
- embeds: float32 [32768, 512], P('cell', 'chan'), may hold values from -260 to 260
Outputs:
- whitened: float32 [32768, 512], P(('cell', 'chan'))
- factor: float32 [512, 512], replicated
All inputs are finite; a program needn't handle non-finite values.
Results may differ from a plain program's by a relative error of at most 0.000088.
Values sent between devices are 32-bit elements; how exact they have to be, the bound alone decides.
No kernel may reach another device: no remote copies, remote signals or barrier semaphores. Data moves between devices by JAX's collectives and lax.ppermute only.
A program may use at most 64 MiB of HBM per device.

v0:
```python
import math
import jax
import jax.numpy as jnp
from jax import lax
from jax.sharding import PartitionSpec as P


def per_device(embeds):
    rows = lax.all_to_all(embeds, "chan", split_axis=0, concat_axis=1, tiled=True)
    partial_value = lax.dot_general(
        rows,
        rows,
        (((0,), (0,)), ((), ())),
        precision=lax.Precision.HIGHEST,
        preferred_element_type=jnp.float32,
    )
    within = lax.psum(partial_value, "cell")
    gram = lax.psum(within, "chan")
    lower = jnp.linalg.cholesky(gram)
    upper = lower.T
    total = rows.shape[0] * lax.axis_size("cell") * lax.axis_size("chan")
    scale = math.sqrt(total)
    whitened = jax.scipy.linalg.solve_triangular(lower, rows.T, lower=True).T * scale
    return (whitened, upper / scale)


def solution(mesh):
    in_specs = (P("cell", "chan"),)
    out_specs = (P(("cell", "chan"), None), P())
    return jax.shard_map(
        per_device, mesh=mesh, in_specs=in_specs, out_specs=out_specs, check_vma=False
    )
```

profile of v0, /device:TPU:0, one launch (start us, length us, event | category | flops | bytes accessed | tf_op | source)
XLA Modules:
  0.0 345.4 jit_solution(12368861745308110171)
XLA Ops:
  7.2 54.7 %all_to_all.19 = f32[4,1024,128]{2,1,0:T(8,128)} all-to-all(f32[4,1024,128]{2,1,0:T(8,128)} %bitcast.65), channel_id=1, replica_groups=mesh['cell'=8,'chan'=4] {'chan'}, dimensions={0} | all-to-all | bytes 4194304 | tf_op jit(solution)/shard_map/all_to_all | solution.py:9
  61.9 1.9 copy.11
  63.8 4.5 %fusion.37 = f32[512,512]{0,1:T(8,128)} fusion(f32[1024,512]{0,1:T(8,128)S(1)} %bitcast.59), kind=kOutput, calls=%fused_computation.71 | convolution fusion | flops 3221225472 | bytes 3145728 | tf_op jit(solution)/shard_map/dot_general | solution.py:10
  68.3 0.5 all-reduce.6.cloned.1.call-start
  68.8 55.6 %all-reduce.4.cloned.1.call-done = f32[512,512]{0,1:T(8,128)} async-done(((f32[512,512]{0,1:T(8,128)}), f32[512,512]{0,1:T(8,128)}) %all-reduce.4.cloned.1.call-update) | async-done | bytes 1048592 | tf_op jit(solution)/shard_map/psum | solution.py:17
  124.4 53.5 %all-reduce.6.cloned.1.call-done = f32[512,512]{0,1:T(8,128)} async-done(((f32[512,512]{0,1:T(8,128)}), f32[512,512]{0,1:T(8,128)}) %all-reduce.6.cloned.1.call-update) | async-done | bytes 1048592 | tf_op jit(solution)/shard_map/psum | solution.py:18
  177.9 2.6 copy.13
  180.5 1.4 fusion.13
  182.0 1.0 copy-done.1
  183.0 11.7 %cholesky.104 = f32[128,128]{1,0:T(8,128)S(1)} custom-call(f32[128,128]{1,0:T(8,128)S(1)} %cholesky.266), custom_call_target="Cholesky" | custom-call | tf_op jit(solution)/shard_map/jit(cholesky)/cholesky | solution.py:19
  194.7 9.8 %custom-call.31 = f32[1,128,128]{1,2,0:T(8,128)S(1)} custom-call(f32[1,128,128]{2,1,0:T(8,128)S(1)} %get-tuple-element.37), custom_call_target="InvertDiagBlocksLowerTriangular" | custom-call | tf_op jit(solution)/shard_map/jit(cholesky)/cholesky | solution.py:19
  204.5 0.1 cholesky.224
  204.6 1.2 constant_dynamic-update-slice_fusion.3
  205.9 1.3 convolution_subtract_fusion.2
  207.2 11.7 %cholesky.217 = f32[128,128]{1,0:T(8,128)S(1)} custom-call(f32[128,128]{1,0:T(8,128)S(1)} %cholesky.270), custom_call_target="Cholesky" | custom-call | tf_op jit(solution)/shard_map/jit(cholesky)/cholesky | solution.py:19
  218.9 9.9 %custom-call.32 = f32[1,128,128]{1,2,0:T(8,128)S(1)} custom-call(f32[1,128,128]{2,1,0:T(8,128)S(1)} %get-tuple-element.34), custom_call_target="InvertDiagBlocksLowerTriangular" | custom-call | tf_op jit(solution)/shard_map/jit(cholesky)/cholesky | solution.py:19
  228.9 0.3 convolution_dynamic-update-slice_fusion
  229.1 1.3 convolution_subtract_fusion.3
  230.4 11.7 %cholesky.238 = f32[128,128]{1,0:T(8,128)S(1)} custom-call(f32[128,128]{1,0:T(8,128)S(1)} %cholesky.275), custom_call_target="Cholesky" | custom-call | tf_op jit(solution)/shard_map/jit(cholesky)/cholesky | solution.py:19
  242.2 0.7 compare_reduce_fusion.1
  242.9 9.8 %custom-call.33 = f32[1,128,128]{1,2,0:T(8,128)S(1)} custom-call(f32[1,128,128]{2,1,0:T(8,128)S(1)} %get-tuple-element.31), custom_call_target="InvertDiagBlocksLowerTriangular" | custom-call | tf_op jit(solution)/shard_map/jit(cholesky)/cholesky | solution.py:19
  252.7 0.2 convolution_dynamic-update-slice_fusion.1
  252.9 1.2 convolution_subtract_fusion.4
  254.2 11.7 %cholesky.255 = f32[128,128]{1,0:T(8,128)S(1)} custom-call(f32[128,128]{1,0:T(8,128)S(1)} %convolution_subtract_fusion.4), custom_call_target="Cholesky" | custom-call | tf_op jit(solution)/shard_map/jit(cholesky)/cholesky | solution.py:19
  265.9 0.6 compare_reduce_fusion
  266.6 0.6 compare_reduce_fusion.2
  269.7 1.8 multiply_bitcast_fusion
  271.5 2.5 copy.15
  274.1 14.4 %while.1 = (s32[]{:T(128)}, f32[512,512]{1,0:T(8,128)}, s32[4,2]{0,1:T(2,128)S(1)}, f32[4,128,128]{2,1,0:T(8,128)}, s32[]{:T(128)}) while((s32[]{:T(128)}, f32[512,512]{1,0:T(8,128)}, s32[4,2]{0,1:T(2,128)S(1)}, f32[4,128,128]{2,1,0:T(8,128)}, s32[]{:T(128)}) %tuple.35), condition=%wide.while_cond, body=%wide.while_body.sunk | while | flops 2 | bytes 132205 | solution.py:23
  274.1 0.1 constant_dynamic-slice_fusion.2
  274.2 0.6 fusion.46
  274.7 3.0 bitcast_dynamic-update-slice_fusion.2
  277.8 0.6 fusion.46
  278.4 3.0 bitcast_dynamic-update-slice_fusion.2
  281.4 0.6 fusion.46
  282.0 3.0 bitcast_dynamic-update-slice_fusion.2
  285.0 0.6 fusion.46
  285.6 2.9 bitcast_dynamic-update-slice_fusion.2
  288.5 40.1 %custom-call.34 = f32[4,128,128]{1,2,0:T(8,128)S(1)} custom-call(f32[4,128,128]{2,1,0:T(8,128)} %get-tuple-element.9), custom_call_target="InvertDiagBlocksLowerTriangular" | custom-call | tf_op jit(solution)/shard_map/jit(_solve_triangular)/triangular_solve | solution.py:23
  328.6 0.6 fusion.15
  329.3 1.4 convolution_subtract_fusion.1
  330.7 0.6 fusion.28
  331.3 1.6 convolution_subtract_fusion
  333.0 0.6 fusion.26
  333.6 2.0 fusion.7
  335.7 0.6 fusion.25
  336.3 0.2 fusion
  336.5 1.8 copy.14
  (19 shorter events, 0.5 us)
Async XLA Ops:
  7.2 117.2 %all-reduce.4.cloned.1.call-start = ((), (), s32[]{:S(2)}) async-start(), calls=%async_computation.1 | async-start | bytes 2097152 | tf_op jit(solution)/shard_map/psum | solution.py:17
  68.3 109.6 %all-reduce.6.cloned.1.call-start = ((), (), s32[]{:S(2)}) async-start(), calls=%async_computation.2 | async-start | bytes 2097152 | tf_op jit(solution)/shard_map/psum | solution.py:18
  177.9 2.6 copy-start
  182.0 1.0 copy-start.1
Sparse Core Ops, SparseCore 0:
  68.4 55.9 all-reduce.3
  126.7 51.1 all-reduce.5
where the time goes:
time: 350 us; the launch traced here: 345 us
  other arithmetic  122 us (35%)
  waiting for transfers between devices  109 us (31%)
  blocking collectives  54.7 us (16%)
  local copies, waits for them, and re-layouts  24.4 us (7%)
  matrix products  17.5 us (5%)
  between operations  17 us (5%)
    another operation x14, other arithmetic, per_device(): lower = jnp.linalg.cholesky(gram)  78.5 us
    psum x1, waiting for transfers between devices, per_device(): within = lax.psum(partial_value, 'cell')  55.6 us
    all_to_all x1, blocking collectives, per_device(): lax.all_to_all(embeds, 'chan', split_axis=0, concat_axis=1, tiled=True)  54.7 us
    psum x1, waiting for transfers between devices, per_device(): gram = lax.psum(within, 'chan')  53.5 us
    another operation x2, other arithmetic, per_device(): jax.scipy.linalg.solve_triangular(lower, rows.T, lower=True).T * scale  40.1 us
    another operation x12, local copies, waits for them, and re-layouts  14.4 us
    another operation x7, matrix products, per_device(): jax.scipy.linalg.solve_triangular(lower, rows.T, lower=True).T * scale  7.6 us
  transfers between devices with their start and end apart: 2, of which 2 were waited for; matrix products, arithmetic and copies ran while one was open for 0% of the time, Pallas kernels for 0%

commit v1 on v0

--- a/solution.py
+++ b/solution.py
@@ -6,7 +6,10 @@
 
 
 def per_device(embeds):
-    rows = lax.all_to_all(embeds, "chan", split_axis=0, concat_axis=1, tiled=True)
+    rows = jnp.concatenate(
+        lax.all_to_all(jnp.stack(jnp.split(embeds, lax.axis_size("chan"), axis=0)), "chan", 0, 0),
+        axis=1,
+    )
     partial_value = lax.dot_general(
         rows,
         rows,

time: 350 us -> 351 us (level)
  no operation moved by 1% of the time
where the time goes in v1:
time: 351 us; the launch traced here: 346 us
  other arithmetic  122 us (35%)
  waiting for transfers between devices  109 us (31%)
  blocking collectives  54.3 us (15%)
  local copies, waits for them, and re-layouts  24.9 us (7%)
  matrix products  17.5 us (5%)
  between operations  17 us (5%)
    another operation x14, other arithmetic, per_device(): lower = jnp.linalg.cholesky(gram)  78.5 us
    psum x1, waiting for transfers between devices, per_device(): within = lax.psum(partial_value, 'cell')  55.6 us
    all_to_all x1, blocking collectives, per_device(): lax.all_to_all(jnp.stack(jnp.split(embeds, lax.axis_size('chan'), axis=0)...  54.3 us
    psum x1, waiting for transfers between devices, per_device(): gram = lax.psum(within, 'chan')  53.5 us
    another operation x2, other arithmetic, per_device(): jax.scipy.linalg.solve_triangular(lower, rows.T, lower=True).T * scale  40.1 us
    another operation x12, local copies, waits for them, and re-layouts  14.4 us
    another operation x7, matrix products, per_device(): jax.scipy.linalg.solve_triangular(lower, rows.T, lower=True).T * scale  7.6 us
  transfers between devices with their start and end apart: 2, of which 2 were waited for; matrix products, arithmetic and copies ran while one was open for 0% of the time, Pallas kernels for 0%

profile of v1, /device:TPU:0, one launch (start us, length us, event | category | flops | bytes accessed | tf_op | source)
XLA Modules:
  0.0 345.8 jit_solution(10953714847248413214)
XLA Ops:
  7.2 1.7 fusion.37
  8.9 0.2 copy.16
  9.1 0.2 copy.18
  9.8 54.3 %all_to_all.5 = f32[4,1024,128]{1,2,0:T(8,128)S(1)} all-to-all(f32[4,1024,128]{1,2,0:T(8,128)S(1)} %pad_maximum_fusion), channel_id=1, replica_groups=mesh['cell'=8,'chan'=4] {'chan'}, dimensions={0} | all-to-all | bytes 4194304 | tf_op jit(solution)/shard_map/all_to_all | solution.py:10
  64.2 4.5 %fusion.38 = f32[512,512]{0,1:T(8,128)} fusion(f32[1024,512]{0,1:T(8,128)S(1)} %bitcast.63), kind=kOutput, calls=%fused_computation.73 | convolution fusion | flops 3221225472 | bytes 3145728 | tf_op jit(solution)/shard_map/dot_general | solution.py:13
  68.7 0.5 all-reduce.6.cloned.1.call-start
  69.2 55.6 %all-reduce.4.cloned.1.call-done = f32[512,512]{0,1:T(8,128)} async-done(((f32[512,512]{0,1:T(8,128)}), f32[512,512]{0,1:T(8,128)}) %all-reduce.4.cloned.1.call-update) | async-done | bytes 1048592 | tf_op jit(solution)/shard_map/psum | solution.py:20
  124.8 53.5 %all-reduce.6.cloned.1.call-done = f32[512,512]{0,1:T(8,128)} async-done(((f32[512,512]{0,1:T(8,128)}), f32[512,512]{0,1:T(8,128)}) %all-reduce.6.cloned.1.call-update) | async-done | bytes 1048592 | tf_op jit(solution)/shard_map/psum | solution.py:21
  178.3 2.6 copy.12
  180.9 1.4 fusion.13
  182.4 1.0 copy-done.1
  183.4 11.7 %cholesky.104 = f32[128,128]{1,0:T(8,128)S(1)} custom-call(f32[128,128]{1,0:T(8,128)S(1)} %cholesky.266), custom_call_target="Cholesky" | custom-call | tf_op jit(solution)/shard_map/jit(cholesky)/cholesky | solution.py:22
  195.1 9.8 %custom-call.31 = f32[1,128,128]{1,2,0:T(8,128)S(1)} custom-call(f32[1,128,128]{2,1,0:T(8,128)S(1)} %get-tuple-element.39), custom_call_target="InvertDiagBlocksLowerTriangular" | custom-call | tf_op jit(solution)/shard_map/jit(cholesky)/cholesky | solution.py:22
  205.0 1.2 constant_dynamic-update-slice_fusion.3
  206.3 1.3 convolution_subtract_fusion.2
  207.6 11.7 %cholesky.217 = f32[128,128]{1,0:T(8,128)S(1)} custom-call(f32[128,128]{1,0:T(8,128)S(1)} %cholesky.270), custom_call_target="Cholesky" | custom-call | tf_op jit(solution)/shard_map/jit(cholesky)/cholesky | solution.py:22
  219.3 9.9 %custom-call.32 = f32[1,128,128]{1,2,0:T(8,128)S(1)} custom-call(f32[1,128,128]{2,1,0:T(8,128)S(1)} %get-tuple-element.36), custom_call_target="InvertDiagBlocksLowerTriangular" | custom-call | tf_op jit(solution)/shard_map/jit(cholesky)/cholesky | solution.py:22
  229.3 0.3 convolution_dynamic-update-slice_fusion
  229.5 1.3 convolution_subtract_fusion.3
  230.8 11.7 %cholesky.238 = f32[128,128]{1,0:T(8,128)S(1)} custom-call(f32[128,128]{1,0:T(8,128)S(1)} %cholesky.275), custom_call_target="Cholesky" | custom-call | tf_op jit(solution)/shard_map/jit(cholesky)/cholesky | solution.py:22
  242.6 0.7 compare_reduce_fusion.1
  243.3 9.8 %custom-call.33 = f32[1,128,128]{1,2,0:T(8,128)S(1)} custom-call(f32[1,128,128]{2,1,0:T(8,128)S(1)} %get-tuple-element.33), custom_call_target="InvertDiagBlocksLowerTriangular" | custom-call | tf_op jit(solution)/shard_map/jit(cholesky)/cholesky | solution.py:22
  253.1 0.2 convolution_dynamic-update-slice_fusion.1
  253.3 1.2 convolution_subtract_fusion.4
  254.6 11.7 %cholesky.255 = f32[128,128]{1,0:T(8,128)S(1)} custom-call(f32[128,128]{1,0:T(8,128)S(1)} %convolution_subtract_fusion.4), custom_call_target="Cholesky" | custom-call | tf_op jit(solution)/shard_map/jit(cholesky)/cholesky | solution.py:22
  266.3 0.6 compare_reduce_fusion
  266.9 0.6 compare_reduce_fusion.2
  270.1 1.8 multiply_bitcast_fusion
  271.9 2.5 copy.14
  274.5 14.4 %while.1 = (s32[]{:T(128)}, f32[512,512]{1,0:T(8,128)}, s32[4,2]{0,1:T(2,128)S(1)}, f32[4,128,128]{2,1,0:T(8,128)}, s32[]{:T(128)}) while((s32[]{:T(128)}, f32[512,512]{1,0:T(8,128)}, s32[4,2]{0,1:T(2,128)S(1)}, f32[4,128,128]{2,1,0:T(8,128)}, s32[]{:T(128)}) %tuple.37), condition=%wide.while_cond, body=%wide.while_body.sunk | while | flops 2 | bytes 132205 | solution.py:26
  274.5 0.6 fusion.47
  275.1 3.0 bitcast_dynamic-update-slice_fusion.2
  278.2 0.6 fusion.47
  278.8 3.0 bitcast_dynamic-update-slice_fusion.2
  281.8 0.6 fusion.47
  282.4 3.0 bitcast_dynamic-update-slice_fusion.2
  285.4 0.6 fusion.47
  286.0 2.9 bitcast_dynamic-update-slice_fusion.2
  288.9 40.1 %custom-call.34 = f32[4,128,128]{1,2,0:T(8,128)S(1)} custom-call(f32[4,128,128]{2,1,0:T(8,128)} %get-tuple-element.9), custom_call_target="InvertDiagBlocksLowerTriangular" | custom-call | tf_op jit(solution)/shard_map/jit(_solve_triangular)/triangular_solve | solution.py:26
  329.0 0.6 fusion.15
  329.7 1.4 convolution_subtract_fusion.1
  331.1 0.6 fusion.28
  331.7 1.6 convolution_subtract_fusion
  333.4 0.6 fusion.26
  334.0 2.0 fusion.7
  336.1 0.6 fusion.25
  336.7 0.2 fusion
  336.9 1.8 copy.13
  (24 shorter events, 1.2 us)
Async XLA Ops:
  7.2 117.6 %all-reduce.4.cloned.1.call-start = ((), (), s32[]{:S(2)}) async-start(), calls=%async_computation.1 | async-start | bytes 2097152 | tf_op jit(solution)/shard_map/psum | solution.py:20
  68.7 109.6 %all-reduce.6.cloned.1.call-start = ((), (), s32[]{:S(2)}) async-start(), calls=%async_computation.2 | async-start | bytes 2097152 | tf_op jit(solution)/shard_map/psum | solution.py:21
  178.3 2.6 copy-start
  182.4 1.0 copy-start.1
Sparse Core Ops, SparseCore 0:
  68.8 55.9 all-reduce.3
  127.1 51.1 all-reduce.5
